TPU v7x, 256 devices: a whole 4x4x8 slice. The times are simulated.
256 devices in a mesh: dp: 16 (over z, core), expert: 16 (over y, x).
Axes of the slice: x: 4, y: 4, z: 8, core: 2. Of those that a mesh axis runs over, the one named last changes fastest.
Arguments:
- tokens: bfloat16 [32768, 1024], P(('dp', 'expert')), may hold values from -6 to 6
- routes: int32 [32768, 8], P(('dp', 'expert')), may hold values from 0 to 63, all different within a row; in each aligned block of 128 rows (0 to 127, 128 to 255, ...) at most 24 rows name the same one
- gates: float32 [32768, 8], P(('dp', 'expert')), may hold values from 0.02 to 0.3
- cotangent: bfloat16 [32768, 1024], P(('dp', 'expert')), may hold values from -6 to 6
- w_gate: bfloat16 [64, 1024, 384], P('expert', 'dp'), may hold values from -0.1875 to 0.1875
- w_up: bfloat16 [64, 1024, 384], P('expert', 'dp'), may hold values from -0.1875 to 0.1875
- w_down: bfloat16 [64, 384, 1024], P('expert', None, 'dp'), may hold values from -0.3125 to 0.3125
Outputs:
- mixed: bfloat16 [32768, 1024], P(('dp', 'expert'))
- input_grad: bfloat16 [32768, 1024], P(('dp', 'expert'))
- gate_grads: float32 [32768, 8], P(('dp', 'expert'))
- grad_gate: float32 [64, 1024, 384], P('expert', 'dp')
- grad_up: float32 [64, 1024, 384], P('expert', 'dp')
- grad_down: float32 [64, 384, 1024], P('expert', None, 'dp')
Inputs may be any that keep to these rules, and one draw needn't show every extreme that they name: `routes`: each row names 8 different experts; within the rows of one device no expert is named more than 24 times, a bound that some block reaches.
All inputs are finite; a program needn't handle non-finite values.
Results may differ from a plain program's by a relative error of at most 0.02.
Values may be sent and summed in bfloat16 or wider, within the bound.
A program may use at most 128 MiB of HBM per device.

v0:
```python
import jax
import jax.numpy as jnp
from jax import lax
from jax.experimental import pallas as pl
from jax.experimental.pallas import tpu as pltpu
from jax.sharding import PartitionSpec as P

BF16 = jnp.bfloat16
F32 = jnp.float32
D, H, TOK, CAP = 1024, 384, 128, 24
NZ, NY, NX = 8, 4, 4
NE = 4
NP = 8
PAIR_ROWS = 2 * CAP
ROWS = 16 * CAP
WID = 3 * H
PART = TOK // 2
MESH = pl.DeviceIdType.MESH
OFFSETS = (0, -1, 1, 2)

(
    OWN,
    FORTH,
    BACK,
    FAR,
    PLUS,
    MINUS,
    W_OWN,
    W_UP,
    W_DOWN,
    W_FAR,
    META,
    SELECT_X,
    SELECT_C,
    FWD,
    BWD_A,
    BWD_B,
    PAIR_A,
    PAIR_B,
    RING_UP,
    RING_DOWN,
    RING_END,
    SUM_UP,
    SUM_DOWN,
    SUM_OWN,
    LAST_UP,
    LAST_DOWN,
    LAST,
    MIX,
    IGRAD,
    TURN,
) = range(30)
TA, TB, CA, CB = range(4)

ORDER = (
    (OWN, TB), (OWN, TA), (W_OWN, 1), (W_OWN, 3), (MINUS, TB, 0), (W_UP, 1, 1), (FORTH, TB),
    (OWN, CA), (W_OWN, 0), (BACK, TB), (BACK, TA), (W_DOWN, 3, 1), (FAR, TB), (W_DOWN, 0, 1),
    (W_UP, 3, 1), (OWN, CB), (PLUS, TA, 0), (FORTH, TA), (W_OWN, 2), (W_DOWN, 3, 2),
    (MINUS, TA, 0), (W_UP, 0, 1), (W_DOWN, 0, 2), (FORTH, CB), (PLUS, TB, 0), (MINUS, CA, 0),
    (W_DOWN, 1, 1), (MINUS, TB, 1), (W_UP, 3, 2), (BACK, CA), (FAR, TA), (BACK, CB), (FORTH, CA),
    (PLUS, TB, 2), (PLUS, TA, 1), (W_UP, 0, 2), (MINUS, CB, 1), (MINUS, TA, 1), (PLUS, TB, 3),
    (MINUS, TB, 2), (PLUS, TA, 3), (W_DOWN, 0, 3), (W_UP, 3, 3), (MINUS, TB, 3), (W_UP, 2, 1),
    (W_DOWN, 3, 3), (PLUS, TB, 1), (FAR, CB), (W_DOWN, 2, 1), (PLUS, CB, 0), (W_DOWN, 1, 2),
    (MINUS, TA, 3), (W_UP, 0, 3), (PLUS, TA, 2), (MINUS, TA, 2), (FAR, CA), (PLUS, CA, 2),
    (MINUS, CB, 0), (PLUS, CB, 1), (W_FAR, 3), (W_UP, 1, 2), (MINUS, CA, 2), (PLUS, CB, 2),
    (W_UP, 2, 2), (META,), (W_DOWN, 2, 2), (PLUS, CA, 0), (SELECT_X,), (MINUS, CB, 2), (W_FAR, 0),
    (PLUS, CB, 3), (MINUS, CA, 1), (PLUS, CA, 3), (FWD, 3), (MINUS, CB, 3), (W_UP, 1, 3),
    (PLUS, CA, 1), (W_DOWN, 1, 3), (MINUS, CA, 3), (TURN,), (FWD, 0), (W_DOWN, 2, 3), (W_UP, 2, 3),
    (SELECT_C,), (W_FAR, 1), (BWD_A, 0), (W_FAR, 2), (BWD_A, 3), (BWD_B, 0), (BWD_B, 3), (FWD, 1),
    (PAIR_A, 0), (FWD, 2), (PAIR_A, 3), (MIX,), (PAIR_B, 0), (RING_UP, 0, 1), (RING_DOWN, 0, 1),
    (BWD_A, 2), (BWD_B, 2), (PAIR_B, 3), (RING_DOWN, 3, 1), (RING_UP, 3, 1), (BWD_A, 1),
    (BWD_B, 1), (RING_DOWN, 0, 2), (RING_UP, 0, 2), (PAIR_A, 2), (RING_DOWN, 3, 2),
    (RING_UP, 3, 2), (IGRAD,), (PAIR_B, 1), (RING_UP, 0, 3), (SUM_UP, TB), (RING_DOWN, 0, 3),
    (PAIR_B, 2), (SUM_DOWN, TA), (RING_UP, 3, 3), (RING_DOWN, 3, 3), (SUM_DOWN, TB), (PAIR_A, 1),
    (SUM_UP, TA), (SUM_UP, CB), (RING_UP, 2, 1), (SUM_UP, CA), (SUM_DOWN, CA), (RING_DOWN, 2, 1),
    (RING_END, 0), (RING_END, 3), (RING_UP, 1, 1), (RING_DOWN, 1, 1), (RING_DOWN, 2, 2),
    (RING_UP, 2, 2), (SUM_DOWN, CB), (SUM_OWN, TB), (RING_DOWN, 1, 2), (RING_UP, 1, 2),
    (SUM_OWN, TA), (RING_UP, 2, 3), (RING_DOWN, 2, 3), (SUM_OWN, CA), (SUM_OWN, CB), (LAST_UP, TA),
    (RING_UP, 1, 3), (LAST_UP, TB), (RING_DOWN, 1, 3), (LAST_DOWN, TB), (LAST_DOWN, TA),
    (LAST_DOWN, CA), (LAST_UP, CA), (LAST_DOWN, CB), (RING_END, 2), (LAST_UP, CB), (LAST, TB),
    (LAST, TA), (RING_END, 1), (LAST, CB), (LAST, CA),
)


def dot_nt(a, b):
    return lax.dot_general(a, b, (((1,), (1,)), ((), ())), preferred_element_type=F32)


def dot_tn(a, b):
    return lax.dot_general(a, b, (((0,), (0,)), ((), ())), preferred_element_type=F32)


def dot_nn(a, b):
    return lax.dot_general(a, b, (((1,), (0,)), ((), ())), preferred_element_type=F32)


def kernel(
    tok_ref, cot_ref, wg_ref, wu_ref, wd_ref, routes_ref, gates_ref,
    mixed_ref, igrad_ref, gg_ref, out_gate, out_up, out_down,
    xbuf, cbuf, wbuf, mbuf, slot, gate, onehot, weighted, hot_t, weighted_t, xe, se, lin, hid, both_ref, orow, rrow, gsend, grecv,
    pr, ru1, rd1, ru, rd, a1, a2, b1, b2, fout, gout,
    send_sems, recv_sems, msend, mrecv, gsem_s, gsem_r, local_sems, out_sems,
):
    dp, ex = lax.axis_index("dp"), lax.axis_index("expert")
    z, c = lax.div(dp, 2), lax.rem(dp, 2)
    y, x = lax.div(ex, NX), lax.rem(ex, NX)
    sibling = (2 * z + (1 - c), ex)

    def mod(a, n):
        return lax.rem(a + n, n)

    def zdev(o):
        return (2 * mod(z + o, NZ) + c, ex)

    def zpos(o):
        return 2 * mod(z + o, NZ) + c

    def plane(oy, ox):
        return mod(y + oy, NY) * NX + mod(x + ox, NX)

    def plane_dev(oy, ox):
        return (dp, plane(oy, ox))

    barrier = pltpu.get_barrier_semaphore()

    def greet(i, _):
        pl.semaphore_signal(barrier, inc=1, device_id=(dp, lax.rem(ex + i, 16)), device_id_type=MESH)
        return 0

    lax.fori_loop(1, 16, greet, 0)
    for dev in (sibling, zdev(1), zdev(-1)):
        pl.semaphore_signal(barrier, inc=1, device_id=dev, device_id_type=MESH)
    local = [
        pltpu.make_async_copy(tok_ref, xbuf.at[ex], local_sems.at[0]),
        pltpu.make_async_copy(cot_ref, cbuf.at[ex], local_sems.at[1]),
        pltpu.make_async_copy(wg_ref, wbuf.at[:, dp, :, pl.ds(0, H)], local_sems.at[2]),
        pltpu.make_async_copy(wu_ref, wbuf.at[:, dp, :, pl.ds(H, H)], local_sems.at[2]),
        pltpu.make_async_copy(wd_ref, wbuf.at[:, dp, :, pl.ds(2 * H, H)], local_sems.at[2]),
    ]
    for copy in local:
        copy.start()
    mbuf[ex, 0:8, :] = routes_ref[...].astype(F32)
    mbuf[ex, 8:16, :] = gates_ref[...]
    gsend[...] = jnp.zeros_like(gsend)
    pl.semaphore_wait(barrier, 18)

    arrivals, departures, pending, actions = {}, {}, {}, {}

    def send(key, src, dst, dev, group):
        copy = pltpu.make_async_remote_copy(
            src_ref=src,
            dst_ref=dst,
            send_sem=send_sems.at[departures.setdefault(group, len(departures))],
            recv_sem=recv_sems.at[arrivals.setdefault(key, len(arrivals))],
            device_id=dev,
            device_id_type=MESH,
        )
        copy.start()
        pending[key] = copy

    def wait(*key):
        pending.pop(key).wait_recv()

    def wait_all(ref, *key):
        pltpu.make_async_copy(ref, ref, recv_sems.at[arrivals[key]]).wait()

    def drain(ref, group):
        pltpu.make_async_copy(ref, ref, send_sems.at[departures[group]]).wait()

    def plane_axes(first):
        if first == "y":
            return (lambda o: plane_dev(o, 0)), (lambda o: plane_dev(0, o)), plane
        return (lambda o: plane_dev(0, o)), (lambda o: plane_dev(o, 0)), (lambda a, b: plane(b, a))

    def gather(n, group, arg, buf, first, lo):
        dev1, dev2, pos = plane_axes(first)
        halves = (pl.ds(lo, PART // 2), pl.ds(lo + PART // 2, PART // 2))

        def move(key, a, b, dev, rows):
            ref = buf.at[pos(a, b), rows]
            send((n,) + key, arg.at[rows] if (a, b) == (0, 0) else ref, ref, dev, group)

        whole = pl.ds(lo, PART)

        def second(i):
            move(("p", i), OFFSETS[i], 0, dev2(1), whole)
            move(("m", i), OFFSETS[i], 0, dev2(-1), whole)

        def own():
            move(("r1p",), 0, 0, dev1(1), whole)
            move(("r1m",), 0, 0, dev1(-1), whole)
            second(0)

        def forward():
            wait(n, "r1p")
            move(("r2",), -1, 0, dev1(1), halves[0])
            second(1)

        def backward():
            wait(n, "r1m")
            move(("r2",), 1, 0, dev1(-1), halves[1])
            second(2)

        def opposite():
            wait_all(buf.at[0, whole], n, "r2")
            second(3)

        def plus(i):
            wait(n, "p", i)
            move(("last",), OFFSETS[i], -1, dev2(1), halves[0])

        def minus(i):
            wait(n, "m", i)
            move(("last",), OFFSETS[i], 1, dev2(-1), halves[1])

        actions[OWN, n] = own
        actions[FORTH, n] = forward
        actions[BACK, n] = backward
        actions[FAR, n] = opposite
        for i in range(4):
            actions[PLUS, n, i] = lambda i=i: plus(i)
            actions[MINUS, n, i] = lambda i=i: minus(i)

    gather(TA, "t", tok_ref, xbuf, "x", 0)
    gather(TB, "t", tok_ref, xbuf, "y", PART)
    gather(CA, "c", cot_ref, cbuf, "x", 0)
    gather(CB, "c", cot_ref, cbuf, "y", PART)

    def gathered(arrays, copy, buf):
        copy.wait()
        for n in arrays:
            wait_all(buf.at[pl.ds(0, 4), pl.ds(0, PART)], n, "last")

    own_weights = [wbuf.at[:, dp]]

    def weight(e):
        def move(key, o, dev, rows=None):
            ref = wbuf.at[e, zpos(o)]
            if rows is not None:
                ref = ref.at[rows]
            send(("w", e) + key, ref, ref, dev, ("w", e))

        def own():
            if own_weights:
                pltpu.make_async_copy(own_weights[0], own_weights.pop(), local_sems.at[2]).wait()
            move(("u", 1), 0, zdev(1))
            move(("d", 1), 0, zdev(-1))
            move(("s",), 0, sibling)

        def up(k):
            wait("w", e, "u", k)
            move(("far",) if k == 3 else ("u", k + 1), -k, zdev(1), pl.ds(0, 32) if k == 3 else None)
            move(("s",), -k, sibling)

        def down(k):
            wait("w", e, "d", k)
            move(("far",) if k == 3 else ("d", k + 1), k, zdev(-1), pl.ds(32, 32) if k == 3 else None)
            move(("s",), k, sibling)

        def opposite():
            wait_all(wbuf.at[e, 0], "w", e, "far")
            move(("s",), 4, sibling)

        actions[W_OWN, e] = own
        actions[W_FAR, e] = opposite
        for k in (1, 2, 3):
            actions[W_UP, e, k] = lambda k=k: up(k)
            actions[W_DOWN, e, k] = lambda k=k: down(k)

    for e in range(NE):
        weight(e)

    def meta_copy(i):
        return pltpu.make_async_remote_copy(
            src_ref=mbuf.at[ex],
            dst_ref=mbuf.at[ex],
            send_sem=msend,
            recv_sem=mrecv,
            device_id=(dp, lax.rem(ex + i, 16)),
            device_id_type=MESH,
        )

    def meta_start(i, _):
        meta_copy(i).start()
        return 0

    def meta():
        for sem in (msend, mrecv):
            pltpu.make_async_copy(mbuf.at[pl.ds(0, 15)], mbuf.at[pl.ds(0, 15)], sem).wait()
        lower = (
            lax.broadcasted_iota(jnp.int32, (TOK, TOK), 0)
            < lax.broadcasted_iota(jnp.int32, (TOK, TOK), 1)
        ).astype(F32).astype(BF16)
        paired = mbuf.reshape(NP, 2, 16, TOK)
        for odd in range(2):
            names = paired[:, odd, 0:8, :]
            values = paired[:, odd, 8:16, :]
            cols = slice(odd * TOK, (odd + 1) * TOK)
            for j in range(NE):
                hit = names == (NE * ex + j).astype(F32)
                member = jnp.max(jnp.where(hit, 1.0, 0.0), axis=1)
                rank = dot_nn(member.astype(BF16), lower)
                slot[j, :, cols] = jnp.where(member > 0.5, rank + float(odd * CAP), -1000.0)
                gate[j, :, cols] = jnp.sum(jnp.where(hit, values, 0.0), axis=1)
        places = lax.broadcasted_iota(jnp.int32, (PAIR_ROWS, 2 * TOK), 0).astype(F32)

        def build(p, _):
            for j in range(NE):
                part = slice(j * PAIR_ROWS, (j + 1) * PAIR_ROWS)
                hit = slot[j, pl.ds(p, 1), :] == places
                onehot[p, part, :] = jnp.where(hit, 1.0, 0.0).astype(BF16)
                weighted[p, part, :] = jnp.where(hit, gate[j, pl.ds(p, 1), :], 0.0).astype(BF16)
            return 0

        lax.fori_loop(0, NP, build, 0)

    actions[(META,)] = meta

    def turn():
        def body(p, _):
            hot_t[p] = onehot[p].T
            weighted_t[p] = weighted[p].T
            return 0

        lax.fori_loop(0, NP, body, 0)

    actions[(TURN,)] = turn

    def pair_at(p):
        return pl.ds(pl.multiple_of(p * PAIR_ROWS, 16), PAIR_ROWS)

    def select_tokens():
        gathered((TA, TB), local[0], xbuf)

        def body(p, _):
            rows = dot_nn(onehot[p], xbuf[pl.ds(2 * p, 2)].reshape(2 * TOK, D)).astype(BF16)
            for j in range(NE):
                xe[j, pair_at(p), :] = rows[j * PAIR_ROWS : (j + 1) * PAIR_ROWS]
            return 0

        lax.fori_loop(0, NP, body, 0, unroll=4)

    def select_cotangent():
        gathered((CA, CB), local[1], cbuf)

        def body(p, _):
            rows = dot_nn(weighted[p], cbuf[pl.ds(2 * p, 2)].reshape(2 * TOK, D)).astype(BF16)
            for j in range(NE):
                se[j, pair_at(p), :] = rows[j * PAIR_ROWS : (j + 1) * PAIR_ROWS]
            return 0

        lax.fori_loop(0, NP, body, 0, unroll=4)

    actions[(SELECT_X,)] = select_tokens
    actions[(SELECT_C,)] = select_cotangent

    def forward(e):
        wait_all(wbuf.at[e, pl.ds(0, 8)], "w", e, "s")
        gate_up = dot_nn(xe[e], wbuf[e, :, :, 0 : 2 * H].reshape(D, 2 * H))
        lin[e] = gate_up
        linear, up = gate_up[:, :H], gate_up[:, H:]
        sig = 1.0 / (1.0 + jnp.exp(-linear))
        hidden = (linear * sig * up).astype(BF16)
        hid[e] = hidden
        out = dot_nt(hidden, wbuf[e, :, :, 2 * H : WID].reshape(D, H))
        orow[:, e * PAIR_ROWS : (e + 1) * PAIR_ROWS, :] = out.astype(BF16).reshape(NP, PAIR_ROWS, D)

    grads = wbuf.reshape(NE, NZ, 2, 64, WID)
    far = 1 - lax.div(z, 4)

    def half_z(o):
        return 4 * lax.rem(far + o, 2)

    def half_grads(e, o):
        q = lax.rem(far + o, 2)
        blocks, cols = pl.ds(8 * q, 8), pl.ds(pl.multiple_of(512 * q, 512), 512)
        both, hidden = both_ref[e], hid[e]
        back = dot_nt(both, wbuf[e, blocks, :, 0 : 2 * H].reshape(512, 2 * H))
        rrow[:, e * PAIR_ROWS : (e + 1) * PAIR_ROWS, cols] = (
            back.astype(BF16).reshape(NP, PAIR_ROWS, 512)
        )
        wbuf[e, blocks, :, 0 : 2 * H] = (
            dot_tn(xe[e, :, cols], both).astype(BF16).reshape(8, 64, 2 * H)
        )
        wbuf[e, blocks, :, 2 * H : WID] = (
            dot_tn(se[e, :, cols], hidden).astype(BF16).reshape(8, 64, H)
        )

    def pair_send(e, o):
        at = half_z(o)
        send(
            ("pair", e, o),
            grads.at[e, pl.ds(at, 4), 1 - c],
            pr.at[e, pl.ds(at, 4)],
            sibling,
            ("z", e),
        )

    def backward_first(e):
        drain(wbuf.at[e, pl.ds(0, 15)], ("w", e))
        hidden_grad = dot_nn(se[e], wbuf[e, :, :, 2 * H : WID].reshape(D, H))
        linear, up = lin[e, :, :H], lin[e, :, H:]
        sig = 1.0 / (1.0 + jnp.exp(-linear))
        up_grad = (hidden_grad * linear * sig).astype(BF16)
        gate_grad = (hidden_grad * up * sig * (1.0 + linear * (1.0 - sig))).astype(BF16)
        products = jnp.sum(hid[e].astype(F32) * hidden_grad, axis=1, keepdims=True)
        for p in range(NP):
            hot = onehot[p, e * PAIR_ROWS : (e + 1) * PAIR_ROWS, :].astype(F32)
            sums = jnp.sum(hot * products[p * PAIR_ROWS : (p + 1) * PAIR_ROWS], axis=0, keepdims=True)
            scale = gate[e, p : p + 1, :].astype(BF16).astype(F32)
            sums = jnp.where(scale > 0.0, sums / jnp.where(scale > 0.0, scale, 1.0), 0.0)
            for odd in range(2):
                gsend[2 * p + odd, e : e + 1, :] = sums[:, odd * TOK : (odd + 1) * TOK]
        both_ref[e, :, :H] = gate_grad
        both_ref[e, :, H:] = up_grad
        half_grads(e, 0)
        pair_send(e, 0)

    def backward_rest(e):
        half_grads(e, 1)
        pair_send(e, 1)

    def add_pair(e, o):
        wait("pair", e, o)
        at = half_z(o)
        for i in range(4):
            pr[e, at + i] = (pr[e, at + i].astype(F32) + grads[e, at + i, c].astype(F32)).astype(BF16)

    def ring_start(e):
        add_pair(e, 0)
        opposite = mod(z + 4, NZ)
        send(("ru", e, 1), pr.at[e, opposite, pl.ds(0, 32)], ru1.at[e], zdev(1), ("z", e))
        send(("rd", e, 1), pr.at[e, opposite, pl.ds(32, 32)], rd1.at[e], zdev(-1), ("z", e))

    def ring_rest(e):
        add_pair(e, 1)

    def ring(e, k, sign):
        name, one, many = ("ru", ru1, ru) if sign == 1 else ("rd", rd1, rd)
        at = mod(z + sign * (4 - k), NZ)
        wait(name, e, k)
        if k == 1:
            rows = pl.ds(0, 32) if sign == 1 else pl.ds(32, 32)
            pr[e, at, rows] = (pr[e, at, rows].astype(F32) + one[e].astype(F32)).astype(BF16)
        else:
            pr[e, at] = (pr[e, at].astype(F32) + many[k - 2, e].astype(F32)).astype(BF16)
        key = ("end", e) if k == 3 else (name, e, k + 1)
        send(key, pr.at[e, at], many.at[k - 1, e], zdev(sign), ("z", e))

    def put(src, dst, k):
        pltpu.make_async_copy(src, dst, out_sems.at[k]).start()

    def ring_end(e):
        wait_all(pr.at[e, pl.ds(0, 2)], "end", e)
        total = pr[e, z].astype(F32) + ru[2, e].astype(F32) + rd[2, e].astype(F32)
        for i, ref in enumerate((out_gate, out_up, out_down)):
            gout[i, e] = total[:, i * H : (i + 1) * H]
            put(gout.at[i, e], ref.at[e], 1)

    for e in range(NE):
        actions[FWD, e] = lambda e=e: forward(e)
        actions[BWD_A, e] = lambda e=e: backward_first(e)
        actions[BWD_B, e] = lambda e=e: backward_rest(e)
        actions[PAIR_A, e] = lambda e=e: ring_start(e)
        actions[PAIR_B, e] = lambda e=e: ring_rest(e)
        actions[RING_END, e] = lambda e=e: ring_end(e)
        for k in (1, 2, 3):
            actions[RING_UP, e, k] = lambda e=e, k=k: ring(e, k, 1)
            actions[RING_DOWN, e, k] = lambda e=e, k=k: ring(e, k, -1)

    def scatter(n, buf, out, first, lo, group_of_sends):
        dev1, dev2, _ = plane_axes(first)
        blocks = buf.reshape(NY, NX, TOK, D)
        whole = pl.ds(lo, PART)
        halves = (pl.ds(lo, PART // 2), pl.ds(lo + PART // 2, PART // 2))
        local_halves = (pl.ds(0, PART // 2), pl.ds(PART // 2, PART // 2))
        mine, other = (y, x) if first == "y" else (x, y)

        def group(o, at, count):
            if first == "y":
                return blocks.at[mod(mine + o, 4), pl.ds(at, count), whole]
            return blocks.at[pl.ds(at, count), mod(mine + o, 4), whole]

        def own(o, rows):
            if first == "y":
                return blocks.at[mine, mod(other + o, 4), rows]
            return blocks.at[mod(other + o, 4), mine, rows]

        def start():
            yield lambda: send((n, "a1p"), group(2, 0, 2), a1.at[n, 0], dev1(1), group_of_sends)
            yield lambda: send((n, "a1m"), group(2, 2, 2), a1.at[n, 1], dev1(-1), group_of_sends)
            yield lambda: send(
                (n, "a2"), group(1, 2, 2), a2.at[n, 0, pl.ds(2, 2)], dev1(1), group_of_sends
            )
            yield lambda: send(
                (n, "a2"), group(-1, 0, 2), a2.at[n, 1, pl.ds(0, 2)], dev1(-1), group_of_sends
            )

        def add(key, k, o, at, name):
            wait(n, key)
            ref = group(o, at, 2)
            for i in range(2):
                ref[i] = (ref[i].astype(F32) + a1[n, k, i].astype(F32)).astype(BF16)
            send((n, name), ref, a2.at[n, k, pl.ds(at, 2)], dev1(o), group_of_sends)

        def total():
            wait_all(a2.at[n], n, "a2")
            for o in (2, 1, -1, 0):
                ref, at = own(o, whole), mod(other + o, 4)
                ref[...] = (
                    ref[...].astype(F32)
                    + a2[n, 0, at].astype(F32)
                    + a2[n, 1, at].astype(F32)
                ).astype(BF16)
                if o == 2:
                    send((n, "b1p"), own(2, halves[0]), b1.at[n, 0], dev2(1), group_of_sends)
                    send((n, "b1m"), own(2, halves[1]), b1.at[n, 1], dev2(-1), group_of_sends)
                if o == 1:
                    send(
                        (n, "b2"), own(1, halves[1]), b2.at[n, 0, local_halves[1]], dev2(1), group_of_sends
                    )
                if o == -1:
                    send(
                        (n, "b2"), own(-1, halves[0]), b2.at[n, 1, local_halves[0]], dev2(-1), group_of_sends
                    )

        def add_second(key, k, o, name):
            wait(n, key)
            ref = own(o, halves[k])
            ref[...] = (ref[...].astype(F32) + b1[n, k].astype(F32)).astype(BF16)
            send((n, name), ref, b2.at[n, k, local_halves[k]], dev2(o), group_of_sends)

        def finish():
            wait_all(b2.at[n], n, "b2")
            fout[n] = (
                own(0, whole)[...].astype(F32)
                + b2[n, 0].astype(F32)
                + b2[n, 1].astype(F32)
            ).astype(BF16)
            put(fout.at[n], out.at[whole], 0)

        actions[SUM_UP, n] = lambda: add("a1p", 0, 1, 0, "a2")
        actions[SUM_DOWN, n] = lambda: add("a1m", 1, -1, 2, "a2")
        actions[SUM_OWN, n] = total
        actions[LAST_UP, n] = lambda: add_second("b1p", 0, 1, "b2")
        actions[LAST_DOWN, n] = lambda: add_second("b1m", 1, -1, "b2")
        actions[LAST, n] = finish
        return start

    starts = {
        "m": (
            scatter(TA, xbuf, mixed_ref, "y", 0, "m"),
            scatter(TB, xbuf, mixed_ref, "x", PART, "m"),
        ),
        "i": (
            scatter(CA, cbuf, igrad_ref, "x", 0, "i"),
            scatter(CB, cbuf, igrad_ref, "y", PART, "i"),
        ),
    }

    def start_sums(n):
        for one, two in zip(starts[n][0](), starts[n][1]()):
            one()
            two()

    def mix():
        drain(xbuf.at[pl.ds(0, 15)], "t")

        def body(p, _):
            mixed = dot_nn(weighted_t[p], orow[p])
            xbuf[pl.ds(2 * p, 2)] = mixed.astype(BF16).reshape(2, TOK, D)
            return 0

        lax.fori_loop(0, NP, body, 0, unroll=4)
        start_sums("m")

    def gg_copy(i):
        return pltpu.make_async_remote_copy(
            src_ref=gsend.at[lax.rem(ex + i, 16)],
            dst_ref=grecv.at[ex],
            send_sem=gsem_s,
            recv_sem=gsem_r,
            device_id=(dp, lax.rem(ex + i, 16)),
            device_id_type=MESH,
        )

    def gg_start(i, _):
        gg_copy(i).start()
        return 0

    def input_grads():
        drain(cbuf.at[pl.ds(0, 15)], "c")

        def body(p, _):
            back = dot_nn(hot_t[p], rrow[p])
            cbuf[pl.ds(2 * p, 2)] = back.astype(BF16).reshape(2, TOK, D)
            return 0

        lax.fori_loop(0, NP, body, 0, unroll=4)
        start_sums("i")
        lax.fori_loop(1, 16, gg_start, 0)

    actions[(MIX,)] = mix
    actions[(IGRAD,)] = input_grads

    lax.fori_loop(1, 16, meta_start, 0)
    for name in ORDER:
        actions[name]()

    for sem in (gsem_s, gsem_r):
        pltpu.make_async_copy(grecv.at[pl.ds(0, 15)], grecv.at[pl.ds(0, 15)], sem).wait()
    grecv[ex] = gsend[ex]
    named = routes_ref[...]
    total = jnp.zeros((8, TOK), F32)
    for owner in range(16):
        for j in range(NE):
            total = total + jnp.where(named == NE * owner + j, grecv[owner, j : j + 1, :], 0.0)
    gg_ref[...] = total
    drain(xbuf.at[pl.ds(0, 15)], "m")
    drain(cbuf.at[pl.ds(0, 15)], "i")
    for e in range(NE):
        drain(wbuf.at[e, pl.ds(0, 15)], ("z", e))
    pltpu.make_async_copy(fout, fout, out_sems.at[0]).wait()
    pltpu.make_async_copy(gout, gout, out_sems.at[1]).wait()


def hand_over(*refs):
    for src, dst in zip(refs[:6], refs[6:]):
        dst[...] = src[...]


def step(tokens, cotangent, w_gate, w_up, w_down, routes, gates):
    any_spec = pl.BlockSpec(memory_space=pl.ANY)
    vmem = pl.BlockSpec(memory_space=pltpu.VMEM)
    out = jax.ShapeDtypeStruct
    shapes = (
        out((TOK, D), BF16),
        out((TOK, D), BF16),
        out((8, TOK), F32),
        out((NE, 64, H), F32),
        out((NE, 64, H), F32),
        out((NE, 64, H), F32),
    )
    mixed, igrad, scores, gate, up, down = pl.pallas_call(
        kernel,
        out_shape=shapes,
        in_specs=[any_spec] * 5 + [vmem] * 2,
        out_specs=(any_spec, any_spec, vmem, any_spec, any_spec, any_spec),
        scratch_shapes=[
            pltpu.VMEM((16, TOK, D), BF16),
            pltpu.VMEM((16, TOK, D), BF16),
            pltpu.VMEM((NE, 16, 64, WID), BF16),
            pltpu.VMEM((16, 16, TOK), F32),
            pltpu.VMEM((NE, NP, 2 * TOK), F32),
            pltpu.VMEM((NE, NP, 2 * TOK), F32),
            pltpu.VMEM((NP, NE * PAIR_ROWS, 2 * TOK), BF16),
            pltpu.VMEM((NP, NE * PAIR_ROWS, 2 * TOK), BF16),
            pltpu.VMEM((NP, 2 * TOK, NE * PAIR_ROWS), BF16),
            pltpu.VMEM((NP, 2 * TOK, NE * PAIR_ROWS), BF16),
            pltpu.VMEM((NE, ROWS, D), BF16),
            pltpu.VMEM((NE, ROWS, D), BF16),
            pltpu.VMEM((NE, ROWS, 2 * H), F32),
            pltpu.VMEM((NE, ROWS, H), BF16),
            pltpu.VMEM((NE, ROWS, 2 * H), BF16),
            pltpu.VMEM((NP, NE * PAIR_ROWS, D), BF16),
            pltpu.VMEM((NP, NE * PAIR_ROWS, D), BF16),
            pltpu.VMEM((16, 8, TOK), F32),
            pltpu.VMEM((16, 8, TOK), F32),
            pltpu.VMEM((NE, NZ, 64, WID), BF16),
            pltpu.VMEM((NE, 32, WID), BF16),
            pltpu.VMEM((NE, 32, WID), BF16),
            pltpu.VMEM((3, NE, 64, WID), BF16),
            pltpu.VMEM((3, NE, 64, WID), BF16),
            pltpu.VMEM((4, 2, 2, PART, D), BF16),
            pltpu.VMEM((4, 2, 4, PART, D), BF16),
            pltpu.VMEM((4, 2, PART // 2, D), BF16),
            pltpu.VMEM((4, 2, PART, D), BF16),
            pltpu.VMEM((4, PART, D), BF16),
            pltpu.VMEM((3, NE, 64, H), F32),
            pltpu.SemaphoreType.DMA((12,)),
            pltpu.SemaphoreType.DMA((4 * 12 + 4 * 8 + 4 * 9 + 4 * 6,)),
            pltpu.SemaphoreType.DMA,
            pltpu.SemaphoreType.DMA,
            pltpu.SemaphoreType.DMA,
            pltpu.SemaphoreType.DMA,
            pltpu.SemaphoreType.DMA((3,)),
            pltpu.SemaphoreType.DMA((2,)),
        ],
        compiler_params=pltpu.CompilerParams(
            collective_id=0, has_side_effects=True, vmem_limit_bytes=64 * 1024 * 1024
        ),
    )(tokens, cotangent, w_gate, w_up, w_down, routes, gates)
    mixed, igrad, scores, gate, up, down = pl.pallas_call(
        hand_over,
        out_shape=shapes,
        in_specs=[vmem] * 6,
        out_specs=(vmem,) * 6,
    )(mixed, igrad, scores, gate, up, down)
    return mixed, igrad, scores, gate, up, down


def body(tokens, routes, gates, cotangent, w_gate, w_up, w_down):
    mixed, igrad, scores, grad_gate, grad_up, grad_down = step(
        tokens, cotangent, w_gate, w_up, jnp.swapaxes(w_down, 1, 2), routes.T, gates.T
    )
    return (mixed, igrad, scores.T, grad_gate, grad_up, jnp.swapaxes(grad_down, 1, 2))


def solution(mesh):
    rows = P(("dp", "expert"), None)
    features = P("expert", "dp", None)
    last = P("expert", None, "dp")
    return jax.shard_map(
        body,
        mesh=mesh,
        in_specs=(rows, rows, rows, rows, features, features, last),
        out_specs=(rows, rows, rows, features, features, last),
        check_vma=False,
    )
```

profile of v0, /device:TPU:2, one launch (start us, length us, event | category | flops | bytes accessed | tf_op | source)
XLA Modules:
  0.0 120.7 jit_solution(12285530243574832473)
XLA Ops:
  0.6 117.5 %shard_map.118 = (bf16[128,1024]{1,0:T(8,128)(2,1)}, bf16[128,1024]{1,0:T(8,128)(2,1)}, f32[8,128]{1,0:T(8,128)}, f32[4,64,384]{2,1,0:T(8,128)}, f32[4,64,384]{2,1,0:T(8,128)}, /*index=5*/f32[4,64,384]{2,1,0:T(8,128)}) custom-call(bf16[128,1024]{1,0:T(8,128)(2,1)} %tok_ref.1, bf16[128,1024]{1,0:T(8,128)(2,1)} %cot_ref.1, bf16[4,64,384]{2,1,0:T(8,128)(2,1)} %wg_ref.1, ...), custom_call_target="tpu_custom_call" | custom-call | tf_op jit(solution)/shard_map/pallas_call | solution.py:644
  118.1 2.6 %shard_map.119 = (bf16[128,1024]{1,0:T(8,128)(2,1)}, bf16[128,1024]{1,0:T(8,128)(2,1)}, f32[8,128]{1,0:T(8,128)}, f32[4,64,384]{2,1,0:T(8,128)}, f32[4,64,384]{2,1,0:T(8,128)}, /*index=5*/f32[4,64,384]{2,1,0:T(8,128)}) custom-call(bf16[128,1024]{1,0:T(8,128)(2,1)} %get-tuple-element.18.refs_0_, bf16[128,1024]{1,0:T(8,128)(2,1)} %get-tuple-element.19.refs_1_, ...), custom_call_target="tpu_custom_call" | custom-call | tf_op jit(solution)/shard_map/pallas_call | solution.py:693
where the time goes:
time: 121 us
  Pallas kernels  120 us (99%)
    pallas_call x1, Pallas kernels, step(): pl.pallas_call(kernel, out_shape=shapes, in_specs=[any_spec] * 5 + [vmem]...  117 us
    pallas_call x1, Pallas kernels, step(): pl.pallas_call(hand_over, out_shape=shapes, in_specs=[vmem] * 6, out_spec...  2.6 us

commit v1 on v0

--- a/solution.py
+++ b/solution.py
@@ -17,6 +17,8 @@
 PART = TOK // 2
 MESH = pl.DeviceIdType.MESH
 OFFSETS = (0, -1, 1, 2)
+PARTS = (4, 2, 2, 2)
+LATER = {2: (1,), 4: (1, 3, 2)}
 
 (
     OWN,
@@ -53,32 +55,33 @@
 TA, TB, CA, CB = range(4)
 
 ORDER = (
-    (OWN, TB), (OWN, TA), (W_OWN, 1), (W_OWN, 3), (MINUS, TB, 0), (W_UP, 1, 1), (FORTH, TB),
-    (OWN, CA), (W_OWN, 0), (BACK, TB), (BACK, TA), (W_DOWN, 3, 1), (FAR, TB), (W_DOWN, 0, 1),
-    (W_UP, 3, 1), (OWN, CB), (PLUS, TA, 0), (FORTH, TA), (W_OWN, 2), (W_DOWN, 3, 2),
-    (MINUS, TA, 0), (W_UP, 0, 1), (W_DOWN, 0, 2), (FORTH, CB), (PLUS, TB, 0), (MINUS, CA, 0),
-    (W_DOWN, 1, 1), (MINUS, TB, 1), (W_UP, 3, 2), (BACK, CA), (FAR, TA), (BACK, CB), (FORTH, CA),
-    (PLUS, TB, 2), (PLUS, TA, 1), (W_UP, 0, 2), (MINUS, CB, 1), (MINUS, TA, 1), (PLUS, TB, 3),
-    (MINUS, TB, 2), (PLUS, TA, 3), (W_DOWN, 0, 3), (W_UP, 3, 3), (MINUS, TB, 3), (W_UP, 2, 1),
-    (W_DOWN, 3, 3), (PLUS, TB, 1), (FAR, CB), (W_DOWN, 2, 1), (PLUS, CB, 0), (W_DOWN, 1, 2),
-    (MINUS, TA, 3), (W_UP, 0, 3), (PLUS, TA, 2), (MINUS, TA, 2), (FAR, CA), (PLUS, CA, 2),
-    (MINUS, CB, 0), (PLUS, CB, 1), (W_FAR, 3), (W_UP, 1, 2), (MINUS, CA, 2), (PLUS, CB, 2),
-    (W_UP, 2, 2), (META,), (W_DOWN, 2, 2), (PLUS, CA, 0), (SELECT_X,), (MINUS, CB, 2), (W_FAR, 0),
-    (PLUS, CB, 3), (MINUS, CA, 1), (PLUS, CA, 3), (FWD, 3), (MINUS, CB, 3), (W_UP, 1, 3),
-    (PLUS, CA, 1), (W_DOWN, 1, 3), (MINUS, CA, 3), (TURN,), (FWD, 0), (W_DOWN, 2, 3), (W_UP, 2, 3),
-    (SELECT_C,), (W_FAR, 1), (BWD_A, 0), (W_FAR, 2), (BWD_A, 3), (BWD_B, 0), (BWD_B, 3), (FWD, 1),
-    (PAIR_A, 0), (FWD, 2), (PAIR_A, 3), (MIX,), (PAIR_B, 0), (RING_UP, 0, 1), (RING_DOWN, 0, 1),
-    (BWD_A, 2), (BWD_B, 2), (PAIR_B, 3), (RING_DOWN, 3, 1), (RING_UP, 3, 1), (BWD_A, 1),
-    (BWD_B, 1), (RING_DOWN, 0, 2), (RING_UP, 0, 2), (PAIR_A, 2), (RING_DOWN, 3, 2),
-    (RING_UP, 3, 2), (IGRAD,), (PAIR_B, 1), (RING_UP, 0, 3), (SUM_UP, TB), (RING_DOWN, 0, 3),
-    (PAIR_B, 2), (SUM_DOWN, TA), (RING_UP, 3, 3), (RING_DOWN, 3, 3), (SUM_DOWN, TB), (PAIR_A, 1),
-    (SUM_UP, TA), (SUM_UP, CB), (RING_UP, 2, 1), (SUM_UP, CA), (SUM_DOWN, CA), (RING_DOWN, 2, 1),
-    (RING_END, 0), (RING_END, 3), (RING_UP, 1, 1), (RING_DOWN, 1, 1), (RING_DOWN, 2, 2),
-    (RING_UP, 2, 2), (SUM_DOWN, CB), (SUM_OWN, TB), (RING_DOWN, 1, 2), (RING_UP, 1, 2),
-    (SUM_OWN, TA), (RING_UP, 2, 3), (RING_DOWN, 2, 3), (SUM_OWN, CA), (SUM_OWN, CB), (LAST_UP, TA),
-    (RING_UP, 1, 3), (LAST_UP, TB), (RING_DOWN, 1, 3), (LAST_DOWN, TB), (LAST_DOWN, TA),
-    (LAST_DOWN, CA), (LAST_UP, CA), (LAST_DOWN, CB), (RING_END, 2), (LAST_UP, CB), (LAST, TB),
-    (LAST, TA), (RING_END, 1), (LAST, CB), (LAST, CA),
+    (W_OWN, 2), (OWN, CA), (OWN, TA), (W_OWN, 0), (W_OWN, 3), (OWN, TB), (W_UP, 0, 1),
+    (MINUS, TA, 0), (BACK, CA), (OWN, CB), (W_DOWN, 0, 1), (W_DOWN, 2, 1), (BACK, TB),
+    (MINUS, TB, 0), (W_DOWN, 3, 1), (BACK, TA), (FORTH, TB), (FORTH, TA), (W_UP, 2, 1), (W_OWN, 1),
+    (W_UP, 0, 2), (FORTH, CB), (BACK, CB), (PLUS, TB, 2), (FAR, TA), (W_DOWN, 2, 2), (W_UP, 2, 2),
+    (PLUS, TA, 2), (PLUS, TB, 1), (FAR, TB), (W_DOWN, 0, 2), (W_UP, 1, 1), (PLUS, TA, 0), (META,),
+    (MINUS, TA, 1), (FORTH, CA), (W_UP, 3, 1), (W_UP, 0, 3), (PLUS, CB, 1), (MINUS, TB, 1),
+    (W_DOWN, 1, 1), (PLUS, TA, 3), (PLUS, TA, 1), (MINUS, TA, 3), (W_DOWN, 2, 3), (W_DOWN, 0, 3),
+    (MINUS, TA, 2), (W_DOWN, 3, 2), (W_UP, 2, 3), (MINUS, TB, 2), (PLUS, TB, 3), (MINUS, TB, 3),
+    (FAR, CA), (PLUS, TB, 0), (MINUS, CA, 1), (FAR, CB), (MINUS, CB, 1), (PLUS, CB, 0),
+    (MINUS, CB, 2), (PLUS, CA, 0), (W_UP, 1, 2), (PLUS, CB, 2), (W_DOWN, 1, 2), (MINUS, CA, 2),
+    (W_FAR, 0), (W_UP, 3, 2), (MINUS, CB, 0), (PLUS, CA, 1), (W_FAR, 2), (SELECT_X,),
+    (MINUS, CA, 0), (PLUS, CA, 3), (PLUS, CA, 2), (MINUS, CB, 3), (TURN,), (W_UP, 1, 3),
+    (W_DOWN, 3, 3), (MINUS, CA, 3), (PLUS, CB, 3), (FWD, 2), (FWD, 0), (W_DOWN, 1, 3),
+    (W_UP, 3, 3), (SELECT_C,), (BWD_A, 0), (W_FAR, 1), (W_FAR, 3), (BWD_B, 0), (PAIR_A, 0),
+    (FWD, 1), (FWD, 3), (PAIR_B, 0), (RING_UP, 0, 1), (RING_DOWN, 0, 1), (MIX,), (BWD_A, 2),
+    (BWD_A, 3), (RING_DOWN, 0, 2), (RING_UP, 0, 2), (BWD_A, 1), (BWD_B, 1), (PAIR_A, 2),
+    (BWD_B, 2), (SUM_DOWN, TB), (PAIR_A, 3), (SUM_UP, TA), (BWD_B, 3), (SUM_UP, TB),
+    (RING_DOWN, 0, 3), (SUM_DOWN, TA), (RING_UP, 0, 3), (PAIR_A, 1), (PAIR_B, 3), (PAIR_B, 1),
+    (RING_UP, 3, 1), (IGRAD,), (RING_DOWN, 3, 1), (PAIR_B, 2), (RING_END, 0), (RING_DOWN, 2, 1),
+    (RING_UP, 2, 1), (RING_DOWN, 3, 2), (RING_UP, 1, 1), (RING_UP, 3, 2), (RING_DOWN, 1, 1),
+    (SUM_DOWN, CB), (SUM_DOWN, CA), (SUM_UP, CB), (RING_UP, 1, 2), (RING_UP, 2, 2),
+    (RING_DOWN, 2, 2), (SUM_UP, CA), (RING_DOWN, 1, 2), (SUM_OWN, TB), (SUM_OWN, TA),
+    (RING_UP, 3, 3), (RING_DOWN, 3, 3), (SUM_OWN, CA), (SUM_OWN, CB), (RING_UP, 2, 3),
+    (RING_DOWN, 2, 3), (LAST_DOWN, TB), (LAST_DOWN, TA), (LAST_UP, TA), (LAST_UP, TB),
+    (RING_UP, 1, 3), (RING_DOWN, 1, 3), (RING_END, 3), (LAST_UP, CB), (LAST_DOWN, CA),
+    (LAST_UP, CA), (LAST_DOWN, CB), (RING_END, 2), (LAST, TA), (LAST, TB), (LAST, CA), (LAST, CB),
+    (RING_END, 1),
 )
 
 
@@ -366,35 +369,30 @@
         orow[:, e * PAIR_ROWS : (e + 1) * PAIR_ROWS, :] = out.astype(BF16).reshape(NP, PAIR_ROWS, D)
 
     grads = wbuf.reshape(NE, NZ, 2, 64, WID)
-    far = 1 - lax.div(z, 4)
-
-    def half_z(o):
-        return 4 * lax.rem(far + o, 2)
-
-    def half_grads(e, o):
-        q = lax.rem(far + o, 2)
-        blocks, cols = pl.ds(8 * q, 8), pl.ds(pl.multiple_of(512 * q, 512), 512)
+    def place(e, o):
+        parts = PARTS[e]
+        span = NZ // parts
+        return lax.rem(lax.div(z, span) + parts // 2 + o, parts)
+
+    def part_grads(e, o):
+        q, n, m = place(e, o), 16 // PARTS[e], D // PARTS[e]
+        blocks, cols = pl.ds(n * q, n), pl.ds(pl.multiple_of(m * q, m), m)
         both, hidden = both_ref[e], hid[e]
-        back = dot_nt(both, wbuf[e, blocks, :, 0 : 2 * H].reshape(512, 2 * H))
+        back = dot_nt(both, wbuf[e, blocks, :, 0 : 2 * H].reshape(m, 2 * H))
         rrow[:, e * PAIR_ROWS : (e + 1) * PAIR_ROWS, cols] = (
-            back.astype(BF16).reshape(NP, PAIR_ROWS, 512)
+            back.astype(BF16).reshape(NP, PAIR_ROWS, m)
         )
         wbuf[e, blocks, :, 0 : 2 * H] = (
-            dot_tn(xe[e, :, cols], both).astype(BF16).reshape(8, 64, 2 * H)
+            dot_tn(xe[e, :, cols], both).astype(BF16).reshape(n, 64, 2 * H)
         )
         wbuf[e, blocks, :, 2 * H : WID] = (
-            dot_tn(se[e, :, cols], hidden).astype(BF16).reshape(8, 64, H)
+            dot_tn(se[e, :, cols], hidden).astype(BF16).reshape(n, 64, H)
         )
 
     def pair_send(e, o):
-        at = half_z(o)
-        send(
-            ("pair", e, o),
-            grads.at[e, pl.ds(at, 4), 1 - c],
-            pr.at[e, pl.ds(at, 4)],
-            sibling,
-            ("z", e),
-        )
+        span = NZ // PARTS[e]
+        at = pl.ds(span * place(e, o), span)
+        send(("pair", e, o > 0), grads.at[e, at, 1 - c], pr.at[e, at], sibling, ("z", e))
 
     def backward_first(e):
         drain(wbuf.at[e, pl.ds(0, 15)], ("w", e))
@@ -413,27 +411,30 @@
                 gsend[2 * p + odd, e : e + 1, :] = sums[:, odd * TOK : (odd + 1) * TOK]
         both_ref[e, :, :H] = gate_grad
         both_ref[e, :, H:] = up_grad
-        half_grads(e, 0)
+        part_grads(e, 0)
         pair_send(e, 0)
 
     def backward_rest(e):
-        half_grads(e, 1)
-        pair_send(e, 1)
-
-    def add_pair(e, o):
-        wait("pair", e, o)
-        at = half_z(o)
-        for i in range(4):
-            pr[e, at + i] = (pr[e, at + i].astype(F32) + grads[e, at + i, c].astype(F32)).astype(BF16)
+        for o in LATER[PARTS[e]]:
+            part_grads(e, o)
+            pair_send(e, o)
+
+    def add_pair(e, parts):
+        span = NZ // PARTS[e]
+        wait_all(pr.at[e, pl.ds(0, span * len(parts))], "pair", e, parts[0] > 0)
+        for o in parts:
+            for i in range(span):
+                at = span * place(e, o) + i
+                pr[e, at] = (pr[e, at].astype(F32) + grads[e, at, c].astype(F32)).astype(BF16)
 
     def ring_start(e):
-        add_pair(e, 0)
+        add_pair(e, (0,))
         opposite = mod(z + 4, NZ)
         send(("ru", e, 1), pr.at[e, opposite, pl.ds(0, 32)], ru1.at[e], zdev(1), ("z", e))
         send(("rd", e, 1), pr.at[e, opposite, pl.ds(32, 32)], rd1.at[e], zdev(-1), ("z", e))
 
     def ring_rest(e):
-        add_pair(e, 1)
+        add_pair(e, LATER[PARTS[e]])
 
     def ring(e, k, sign):
         name, one, many = ("ru", ru1, ru) if sign == 1 else ("rd", rd1, rd)
@@ -690,11 +691,15 @@
             collective_id=0, has_side_effects=True, vmem_limit_bytes=64 * 1024 * 1024
         ),
     )(tokens, cotangent, w_gate, w_up, w_down, routes, gates)
+    rows = pl.BlockSpec((TOK // 2, D), lambda i: (i, 0))
+    experts = pl.BlockSpec((NE // 2, 64, H), lambda i: (i, 0, 0))
+    blocks = (rows, rows, pl.BlockSpec((8, TOK), lambda i: (0, 0)), experts, experts, experts)
     mixed, igrad, scores, gate, up, down = pl.pallas_call(
         hand_over,
+        grid=(2,),
         out_shape=shapes,
-        in_specs=[vmem] * 6,
-        out_specs=(vmem,) * 6,
+        in_specs=blocks,
+        out_specs=blocks,
     )(mixed, igrad, scores, gate, up, down)
     return mixed, igrad, scores, gate, up, down
 

time: 121 us -> 118 us (0.975)
  Pallas kernels: 120 us -> 117 us
    pallas_call x1, Pallas kernels: 117 us -> 115 us  [step(): pl.pallas_call(kernel, out_shape=shapes, in_specs=[any_spec] * 5 + [vmem]...]
where the time goes in v1:
time: 118 us
  Pallas kernels  117 us (99%)
    pallas_call x1, Pallas kernels, step(): pl.pallas_call(kernel, out_shape=shapes, in_specs=[any_spec] * 5 + [vmem]...  115 us
    pallas_call x1, Pallas kernels, step(): pl.pallas_call(hand_over, grid=(2,), out_shape=shapes, in_specs=blocks, o...  2.51 us

profile of v1, /device:TPU:2, one launch (start us, length us, event | category | flops | bytes accessed | tf_op | source)
XLA Modules:
  0.0 118.0 jit_solution(3209736587395855496)
XLA Ops:
  0.6 114.7 %shard_map.118 = (bf16[128,1024]{1,0:T(8,128)(2,1)}, bf16[128,1024]{1,0:T(8,128)(2,1)}, f32[8,128]{1,0:T(8,128)}, f32[4,64,384]{2,1,0:T(8,128)}, f32[4,64,384]{2,1,0:T(8,128)}, /*index=5*/f32[4,64,384]{2,1,0:T(8,128)}) custom-call(bf16[128,1024]{1,0:T(8,128)(2,1)} %tok_ref.1, bf16[128,1024]{1,0:T(8,128)(2,1)} %cot_ref.1, bf16[4,64,384]{2,1,0:T(8,128)(2,1)} %wg_ref.1, ...), custom_call_target="tpu_custom_call" | custom-call | tf_op jit(solution)/shard_map/pallas_call | solution.py:645
  115.3 2.5 %shard_map.119 = (bf16[128,1024]{1,0:T(8,128)(2,1)}, bf16[128,1024]{1,0:T(8,128)(2,1)}, f32[8,128]{1,0:T(8,128)}, f32[4,64,384]{2,1,0:T(8,128)}, f32[4,64,384]{2,1,0:T(8,128)}, /*index=5*/f32[4,64,384]{2,1,0:T(8,128)}) custom-call(bf16[128,1024]{1,0:T(8,128)(2,1)} %get-tuple-element.18.refs_0_, bf16[128,1024]{1,0:T(8,128)(2,1)} %get-tuple-element.19.refs_1_, ...), custom_call_target="tpu_custom_call" | custom-call | tf_op jit(solution)/shard_map/pallas_call | solution.py:697

commit v2 on v1

--- a/solution.py
+++ b/solution.py
@@ -51,7 +51,8 @@
     MIX,
     IGRAD,
     TURN,
-) = range(30)
+    MIX_A,
+) = range(31)
 TA, TB, CA, CB = range(4)
 
 ORDER = (
@@ -69,9 +70,9 @@
     (MINUS, CA, 0), (PLUS, CA, 3), (PLUS, CA, 2), (MINUS, CB, 3), (TURN,), (W_UP, 1, 3),
     (W_DOWN, 3, 3), (MINUS, CA, 3), (PLUS, CB, 3), (FWD, 2), (FWD, 0), (W_DOWN, 1, 3),
     (W_UP, 3, 3), (SELECT_C,), (BWD_A, 0), (W_FAR, 1), (W_FAR, 3), (BWD_B, 0), (PAIR_A, 0),
-    (FWD, 1), (FWD, 3), (PAIR_B, 0), (RING_UP, 0, 1), (RING_DOWN, 0, 1), (MIX,), (BWD_A, 2),
-    (BWD_A, 3), (RING_DOWN, 0, 2), (RING_UP, 0, 2), (BWD_A, 1), (BWD_B, 1), (PAIR_A, 2),
-    (BWD_B, 2), (SUM_DOWN, TB), (PAIR_A, 3), (SUM_UP, TA), (BWD_B, 3), (SUM_UP, TB),
+    (FWD, 1), (FWD, 3), (PAIR_B, 0), (RING_UP, 0, 1), (RING_DOWN, 0, 1), (MIX_A,), (MIX,),
+    (BWD_A, 2), (BWD_A, 3), (RING_DOWN, 0, 2), (RING_UP, 0, 2), (BWD_A, 1), (BWD_B, 1),
+    (PAIR_A, 2), (BWD_B, 2), (SUM_DOWN, TB), (PAIR_A, 3), (SUM_UP, TA), (BWD_B, 3), (SUM_UP, TB),
     (RING_DOWN, 0, 3), (SUM_DOWN, TA), (RING_UP, 0, 3), (PAIR_A, 1), (PAIR_B, 3), (PAIR_B, 1),
     (RING_UP, 3, 1), (IGRAD,), (RING_DOWN, 3, 1), (PAIR_B, 2), (RING_END, 0), (RING_DOWN, 2, 1),
     (RING_UP, 2, 1), (RING_DOWN, 3, 2), (RING_UP, 1, 1), (RING_UP, 3, 2), (RING_DOWN, 1, 1),
@@ -564,15 +565,17 @@
             one()
             two()
 
+    def mix_pair(p, _):
+        mixed = dot_nn(weighted_t[p], orow[p])
+        xbuf[pl.ds(2 * p, 2)] = mixed.astype(BF16).reshape(2, TOK, D)
+        return 0
+
+    def mix_first():
+        drain(xbuf.at[pl.ds(0, 15)], "t")
+        lax.fori_loop(0, NP // 2, mix_pair, 0, unroll=4)
+
     def mix():
-        drain(xbuf.at[pl.ds(0, 15)], "t")
-
-        def body(p, _):
-            mixed = dot_nn(weighted_t[p], orow[p])
-            xbuf[pl.ds(2 * p, 2)] = mixed.astype(BF16).reshape(2, TOK, D)
-            return 0
-
-        lax.fori_loop(0, NP, body, 0, unroll=4)
+        lax.fori_loop(NP // 2, NP, mix_pair, 0, unroll=4)
         start_sums("m")
 
     def gg_copy(i):
@@ -601,6 +604,7 @@
         start_sums("i")
         lax.fori_loop(1, 16, gg_start, 0)
 
+    actions[(MIX_A,)] = mix_first
     actions[(MIX,)] = mix
     actions[(IGRAD,)] = input_grads
 
@@ -626,8 +630,16 @@
 
 
 def hand_over(*refs):
-    for src, dst in zip(refs[:6], refs[6:]):
-        dst[...] = src[...]
+    held, sems = refs[12:18], refs[18]
+    taken = [pltpu.make_async_copy(refs[i], held[i], sems.at[0, i]) for i in range(6)]
+    given = [pltpu.make_async_copy(held[i], refs[6 + i], sems.at[1, i]) for i in range(6)]
+    for copy in taken:
+        copy.start()
+    for into, out in zip(taken, given):
+        into.wait()
+        out.start()
+    for copy in given:
+        copy.wait()
 
 
 def step(tokens, cotangent, w_gate, w_up, w_down, routes, gates):
@@ -691,15 +703,13 @@
             collective_id=0, has_side_effects=True, vmem_limit_bytes=64 * 1024 * 1024
         ),
     )(tokens, cotangent, w_gate, w_up, w_down, routes, gates)
-    rows = pl.BlockSpec((TOK // 2, D), lambda i: (i, 0))
-    experts = pl.BlockSpec((NE // 2, 64, H), lambda i: (i, 0, 0))
-    blocks = (rows, rows, pl.BlockSpec((8, TOK), lambda i: (0, 0)), experts, experts, experts)
     mixed, igrad, scores, gate, up, down = pl.pallas_call(
         hand_over,
-        grid=(2,),
         out_shape=shapes,
-        in_specs=blocks,
-        out_specs=blocks,
+        in_specs=[any_spec] * 6,
+        out_specs=(any_spec,) * 6,
+        scratch_shapes=[pltpu.VMEM(one.shape, one.dtype) for one in shapes]
+        + [pltpu.SemaphoreType.DMA((2, 6))],
     )(mixed, igrad, scores, gate, up, down)
     return mixed, igrad, scores, gate, up, down
 

time: 118 us -> 118 us (level)
  no operation moved by 1% of the time
where the time goes in v2:
time: 118 us
  Pallas kernels  117 us (99%)
    pallas_call x1, Pallas kernels, step(): pl.pallas_call(kernel, out_shape=shapes, in_specs=[any_spec] * 5 + [vmem]...  115 us

profile of v2, /device:TPU:2, one launch (start us, length us, event | category | flops | bytes accessed | tf_op | source)
XLA Modules:
  0.0 117.7 jit_solution(10724974419168498498)
XLA Ops:
  0.6 114.6 %shard_map.118 = (bf16[128,1024]{1,0:T(8,128)(2,1)}, bf16[128,1024]{1,0:T(8,128)(2,1)}, f32[8,128]{1,0:T(8,128)}, f32[4,64,384]{2,1,0:T(8,128)}, f32[4,64,384]{2,1,0:T(8,128)}, /*index=5*/f32[4,64,384]{2,1,0:T(8,128)}) custom-call(bf16[128,1024]{1,0:T(8,128)(2,1)} %tok_ref.1, bf16[128,1024]{1,0:T(8,128)(2,1)} %cot_ref.1, bf16[4,64,384]{2,1,0:T(8,128)(2,1)} %wg_ref.1, ...), custom_call_target="tpu_custom_call" | custom-call | tf_op jit(solution)/shard_map/pallas_call | solution.py:657
  115.2 2.3 %shard_map.119 = (bf16[128,1024]{1,0:T(8,128)(2,1)}, bf16[128,1024]{1,0:T(8,128)(2,1)}, f32[8,128]{1,0:T(8,128)}, f32[4,64,384]{2,1,0:T(8,128)}, f32[4,64,384]{2,1,0:T(8,128)}, /*index=5*/f32[4,64,384]{2,1,0:T(8,128)}) custom-call(bf16[128,1024]{1,0:T(8,128)(2,1)} %get-tuple-element.18.refs_0_, bf16[128,1024]{1,0:T(8,128)(2,1)} %get-tuple-element.19.refs_1_, ...), custom_call_target="tpu_custom_call" | custom-call | tf_op jit(solution)/shard_map/pallas_call | solution.py:706
